TPU v7x, 32 devices: a whole 2x2x4 slice. The times are simulated.
32 devices in a mesh: row: 4 (over y, x), col: 8 (over z, core).
Axes of the slice: x: 2, y: 2, z: 4, core: 2. Of those that a mesh axis runs over, the one named last changes fastest.
Arguments:
- right_side: float32 [512, 128], P('row'), may hold values from -6 to 6
- factor_window: float32 [512, 512], P('row', 'col'), may hold values from -0.1875 to 0.1875
- diag_inverse: float32 [512, 128], P('row'), as said below
- phase_cov: bfloat16 [512, 16384], P('col', 'row'), may hold values from -0.25 to 0.25
Outputs:
- basis: float32 [32, 512, 128], P('row', 'col')
- solved: float32 [512, 128], P('col')
Inputs may be any that keep to these rules, and one draw needn't show every extreme that they name: `diag_inverse`: each block of 128 rows is a lower triangular matrix with a diagonal between 0.5 and 2.
All inputs are finite; a program needn't handle non-finite values.
Results may differ from a plain program's by a relative error of at most 0.0043.
Values sent between devices are 32-bit elements; how exact they have to be, the bound alone decides.
A program may use at most 64 MiB of HBM per device.

v0:
```python
import jax
import jax.numpy as jnp
from jax import lax
from jax.sharding import PartitionSpec as P

TILE_ROWS = 512


def from_root(block, axis, owner):
    block = jnp.where(lax.axis_index(axis) == owner, block, jnp.zeros_like(block))
    return lax.psum(block, axis)


def tile_basis(lower, tile):
    return jax.scipy.linalg.solve_triangular(lower, tile.T, lower=True).T


def finish_tiles(gram, tiles):
    lower = jnp.linalg.cholesky(gram)
    return jax.vmap(tile_basis)(lower, tiles)


def local(right_side, factor_window, diag_inverse, phase_cov):
    row_count = lax.axis_size("row")
    col_count = lax.axis_size("col")
    col_index = lax.axis_index("col")
    block_rows = right_side.shape[0]
    rank_width = right_side.shape[1]
    col_width = factor_window.shape[1]
    col_ratio = col_count // row_count
    row_offset = col_index % col_ratio * col_width
    owner_block = col_index // col_ratio
    partial_value = jnp.zeros((block_rows, rank_width), jnp.float32)
    own_solved = jnp.zeros((col_width, rank_width), jnp.float32)
    for block_index in range(row_count):
        summed = lax.psum(partial_value, "col")
        remaining = right_side - summed
        solved_full = jnp.dot(
            diag_inverse,
            remaining,
            precision=lax.Precision.HIGHEST,
            preferred_element_type=jnp.float32,
        )
        received = from_root(solved_full, "row", block_index)
        column_piece = lax.dynamic_slice_in_dim(received, row_offset, col_width, 0)
        owns_block = owner_block == block_index
        own_solved = jnp.where(owns_block, column_piece, own_solved)
        partial_value = lax.cond(
            owns_block,
            lambda running: running
            + jnp.dot(
                factor_window,
                column_piece,
                precision=lax.Precision.HIGHEST,
                preferred_element_type=jnp.float32,
            ),
            lambda running: running,
            partial_value,
        )
    solved_low = own_solved.astype(jnp.bfloat16)
    tile_count = phase_cov.shape[1] // TILE_ROWS
    cov_tiles = phase_cov.reshape(col_width, tile_count, TILE_ROWS)
    whole_tiles = lax.psum_scatter(
        jnp.einsum("kts,kr->tsr", cov_tiles, solved_low, preferred_element_type=jnp.float32),
        "col",
        scatter_dimension=0,
        tiled=True,
    )
    gram = jnp.einsum("tsr,tsq->trq", whole_tiles, whole_tiles, precision=lax.Precision.HIGHEST)
    tile_bases = finish_tiles(gram, whole_tiles)
    basis = lax.all_to_all(tile_bases, "col", split_axis=1, concat_axis=0, tiled=True)
    return (basis, own_solved)


def solution(mesh):
    in_specs = (P("row", None), P("row", "col"), P("row", None), P("col", "row"))
    out_specs = (P("row", "col", None), P("col", None))
    return jax.shard_map(local, mesh=mesh, in_specs=in_specs, out_specs=out_specs, check_vma=False)
```

profile of v0, /device:TPU:0, one launch (start us, length us, event | category | flops | bytes accessed | tf_op | source)
XLA Modules:
  0.0 444.9 jit_solution(12275134099939349102)
XLA Ops:
  7.2 0.8 copy-done
  8.0 1.7 convolution_select_fusion.3
  9.8 46.2 %all-reduce.8.cloned.1.call-done = f32[128,128]{1,0:T(8,128)} async-done(((f32[128,128]{1,0:T(8,128)}), f32[128,128]{1,0:T(8,128)}) %all-reduce.8.cloned.1.call-update) | async-done | bytes 65552 | tf_op jit(solution)/shard_map/psum | solution.py:11
  56.0 0.8 constant_dynamic-slice_fusion.2
  56.8 1.0 conditional.3
  56.8 1.0 fusion.16
  58.5 55.1 %all-reduce.10.cloned.1.call-done = f32[128,128]{1,0:T(8,128)} async-done(((f32[128,128]{1,0:T(8,128)}), f32[128,128]{1,0:T(8,128)}) %all-reduce.10.cloned.1.call-update) | async-done | bytes 65552 | tf_op jit(solution)/shard_map/psum | solution.py:36
  113.6 1.7 fusion.2
  115.4 42.0 %all-reduce.12.cloned.1.call-done = f32[128,128]{1,0:T(8,128)} async-done(((f32[128,128]{1,0:T(8,128)}), f32[128,128]{1,0:T(8,128)}) %all-reduce.12.cloned.1.call-update) | async-done | bytes 65552 | tf_op jit(solution)/shard_map/psum | solution.py:11
  157.4 0.8 constant_dynamic-slice_fusion.1
  158.2 56.6 %all-reduce.14.cloned.1.call-done = f32[128,128]{1,0:T(8,128)} async-done(((f32[128,128]{1,0:T(8,128)}), f32[128,128]{1,0:T(8,128)}) %all-reduce.14.cloned.1.call-update) | async-done | bytes 65552 | tf_op jit(solution)/shard_map/psum | solution.py:36
  214.9 1.7 fusion.1
  216.7 41.8 %all-reduce.16.cloned.1.call-done = f32[128,128]{1,0:T(8,128)} async-done(((f32[128,128]{1,0:T(8,128)}), f32[128,128]{1,0:T(8,128)}) %all-reduce.16.cloned.1.call-update) | async-done | bytes 65552 | tf_op jit(solution)/shard_map/psum | solution.py:11
  259.3 56.6 %all-reduce.18.cloned.1.call-done = f32[128,128]{1,0:T(8,128)} async-done(((f32[128,128]{1,0:T(8,128)}), f32[128,128]{1,0:T(8,128)}) %all-reduce.18.cloned.1.call-update) | async-done | bytes 65552 | tf_op jit(solution)/shard_map/psum | solution.py:36
  316.0 1.7 fusion
  317.8 42.6 %all-reduce.20.cloned.1.call-done = f32[128,128]{1,0:T(8,128)} async-done(((f32[128,128]{1,0:T(8,128)}), f32[128,128]{1,0:T(8,128)}) %all-reduce.20.cloned.1.call-update) | async-done | bytes 65552 | tf_op jit(solution)/shard_map/psum | solution.py:11
  360.3 0.8 select_select_fusion.1
  361.2 1.8 convolution_bitcast_fusion
  363.0 36.4 %reduce-scatter.2.cloned.1.call-done = f32[1,512,128]{1,2,0:T(8,128)} async-done(((f32[8,512,128]{1,2,0:T(8,128)}), f32[1,512,128]{1,2,0:T(8,128)}) %reduce-scatter.2.cloned.1.call-update) | async-done | bytes 262160 | tf_op jit(solution)/shard_map/reduce_scatter | solution.py:63
  399.3 1.4 fusion.6
  400.9 11.7 %custom-call.8 = f32[1,128,128]{2,1,0:T(8,128)S(1)} custom-call(f32[1,128,128]{2,1,0:T(8,128)S(1)} %fusion.9), custom_call_target="Cholesky" | custom-call | tf_op jit(solution)/shard_map/jit(cholesky)/cholesky | solution.py:19
  413.9 9.8 %custom-call.9 = f32[1,1,128,128]{2,3,1,0:T(8,128)S(1)} custom-call(f32[1,1,128,128]{3,2,1,0:T(8,128)S(1)} %fusion.8), custom_call_target="InvertDiagBlocksLowerTriangular" | custom-call | tf_op jit(solution)/shard_map/vmap(jit(_solve_triangular))/triangular_solve | solution.py:15
  423.7 1.4 convolution_bitcast_fusion.1
  425.2 12.1 %all_to_all.12 = f32[1,512,128]{2,0,1:T(1,128)S(1)} all-to-all(f32[1,512,128]{2,0,1:T(1,128)S(1)} %copy.38), channel_id=1, replica_groups=mesh['row'=4,'col'=8] {'col'}, dimensions={1} | all-to-all | bytes 524288 | tf_op jit(solution)/shard_map/all_to_all | solution.py:71
  (33 shorter events, 4.1 us)
Async XLA Ops:
  7.2 0.8 copy-start
  7.2 354.0 %copy-start.2 = (bf16[64,4096]{1,0:T(8,128)(2,1)S(1)}, bf16[64,4096]{1,0:T(8,128)(2,1)}, u32[]{:S(2)}) copy-start(bf16[64,4096]{1,0:T(8,128)(2,1)} %param.13) | copy-start | bytes 1572868
  7.2 48.8 %all-reduce.8.cloned.1.call-start = ((), (), s32[]{:S(2)}) async-start(), calls=%async_computation.2 | async-start | bytes 131072 | tf_op jit(solution)/shard_map/psum | solution.py:11
  9.7 103.9 %all-reduce.10.cloned.1.call-start = ((), (), s32[]{:S(2)}) async-start(), calls=%async_computation.3 | async-start | bytes 131072 | tf_op jit(solution)/shard_map/psum | solution.py:36
  57.8 0.6 copy-start.1
  58.5 98.9 %all-reduce.12.cloned.1.call-start = ((), (), s32[]{:S(2)}) async-start(), calls=%async_computation.4 | async-start | bytes 131072 | tf_op jit(solution)/shard_map/psum | solution.py:11
  115.4 99.5 %all-reduce.14.cloned.1.call-start = ((), (), s32[]{:S(2)}) async-start(), calls=%async_computation.5 | async-start | bytes 131072 | tf_op jit(solution)/shard_map/psum | solution.py:36
  158.2 100.3 %all-reduce.16.cloned.1.call-start = ((), (), s32[]{:S(2)}) async-start(), calls=%async_computation.6 | async-start | bytes 131072 | tf_op jit(solution)/shard_map/psum | solution.py:11
  216.6 99.4 %all-reduce.18.cloned.1.call-start = ((), (), s32[]{:S(2)}) async-start(), calls=%async_computation.7 | async-start | bytes 131072 | tf_op jit(solution)/shard_map/psum | solution.py:36
  259.3 101.0 %all-reduce.20.cloned.1.call-start = ((), (), s32[]{:S(2)}) async-start(), calls=%async_computation.8 | async-start | bytes 131072 | tf_op jit(solution)/shard_map/psum | solution.py:11
  317.7 81.6 %reduce-scatter.2.cloned.1.call-start = ((), (), s32[]{:S(2)}) async-start(), calls=%async_computation.9 | async-start | bytes 2359296 | tf_op jit(solution)/shard_map/reduce_scatter | solution.py:63
  361.1 1.8 copy-start.3
Sparse Core Ops, SparseCore 0:
  11.4 44.5 all-reduce.7
  58.9 54.6 all-reduce.9
  116.5 40.8 all-reduce.11
  160.1 54.6 all-reduce.13
  217.6 40.8 all-reduce.15
  261.2 54.6 all-reduce.17
  319.4 40.8 all-reduce.19
  363.1 36.2 reduce-scatter.1
where the time goes:
time: 446 us; the launch traced here: 445 us
  waiting for transfers between devices  377 us (85%)
  other arithmetic  23.7 us (5%)
  between operations  14.3 us (3%)
  matrix products  12.4 us (3%)
  blocking collectives  12.1 us (3%)
  local copies, waits for them, and re-layouts  4.6 us (1%)
    psum x4, waiting for transfers between devices, from_root(): return lax.psum(block, axis)  173 us
    psum x3, waiting for transfers between devices, local(): summed = lax.psum(partial_value, 'col')  168 us
    reduce_scatter x1, waiting for transfers between devices, local(): lax.psum_scatter(jnp.einsum('kts,kr->tsr', cov_tiles, solved_low, preferr...  36.4 us
    another operation x3, other arithmetic, finish_tiles(): lower = jnp.linalg.cholesky(gram)  12.4 us
    all_to_all x1, blocking collectives, local(): lax.all_to_all(tile_bases, 'col', split_axis=1, concat_axis=0, tiled=True)  12.1 us
    another operation x2, other arithmetic, tile_basis(): return jax.scipy.linalg.solve_triangular(lower, tile.T, lower=True).T  10.5 us
  transfers between devices with their start and end apart: 8, of which 8 were waited for; matrix products, arithmetic and copies ran while one was open for 0% of the time, Pallas kernels for 0%

commit v1 on v0

--- a/solution.py
+++ b/solution.py
@@ -33,7 +33,10 @@
     partial_value = jnp.zeros((block_rows, rank_width), jnp.float32)
     own_solved = jnp.zeros((col_width, rank_width), jnp.float32)
     for block_index in range(row_count):
-        summed = lax.psum(partial_value, "col")
+        size, summed = (lax.axis_size("col"), partial_value)
+        for reach in [1 << k for k in range(size.bit_length() - 1)]:
+            pairs = [(i, i ^ reach) for i in range(size)]
+            summed = summed + lax.ppermute(summed, "col", pairs)
         remaining = right_side - summed
         solved_full = jnp.dot(
             diag_inverse,

time: 446 us -> 315 us (0.71)
  waiting for transfers between devices: 377 us -> 232 us
  starting transfers between devices: 0.33 us -> 18.2 us
    psum x3 -> x0, waiting for transfers between devices: 168 us -> none  [local(): summed = lax.psum(partial_value, 'col')]
    ppermute x0 -> x12, waiting for transfers between devices: none -> 28.3 us  [local(): summed = summed + lax.ppermute(summed, 'col', pairs)]
    ppermute x0 -> x12, starting transfers between devices: none -> 18 us  [local(): summed = summed + lax.ppermute(summed, 'col', pairs)]
    psum x4, waiting for transfers between devices: 173 us -> 168 us  [from_root(): return lax.psum(block, axis)]
  transfers between devices with their start and end apart: 8 -> 17, of which waited for: 8 -> 17; matrix products, arithmetic and copies ran while one was open for 0% -> 0% of each run, Pallas kernels for 0% -> 0%
where the time goes in v1:
time: 315 us; the launch traced here: 314 us
  waiting for transfers between devices  232 us (74%)
  other arithmetic  23.7 us (8%)
  starting transfers between devices  18.2 us (6%)
  between operations  14 us (4%)
  blocking collectives  12.1 us (4%)
  matrix products  9.88 us (3%)
  local copies, waits for them, and re-layouts  4.3 us (1%)
    psum x4, waiting for transfers between devices, from_root(): return lax.psum(block, axis)  168 us
    reduce_scatter x1, waiting for transfers between devices, local(): lax.psum_scatter(jnp.einsum('kts,kr->tsr', cov_tiles, solved_low, preferr...  36.1 us
    ppermute x12, waiting for transfers between devices, local(): summed = summed + lax.ppermute(summed, 'col', pairs)  28.3 us
    ppermute x12, starting transfers between devices, local(): summed = summed + lax.ppermute(summed, 'col', pairs)  18 us
    another operation x3, other arithmetic, finish_tiles(): lower = jnp.linalg.cholesky(gram)  12.4 us
    all_to_all x1, blocking collectives, local(): lax.all_to_all(tile_bases, 'col', split_axis=1, concat_axis=0, tiled=True)  12.1 us
    another operation x2, other arithmetic, tile_basis(): return jax.scipy.linalg.solve_triangular(lower, tile.T, lower=True).T  10.5 us
  transfers between devices with their start and end apart: 17, of which 17 were waited for; matrix products, arithmetic and copies ran while one was open for 0% of the time, Pallas kernels for 0%

profile of v1, /device:TPU:0, one launch (start us, length us, event | category | flops | bytes accessed | tf_op | source)
XLA Modules:
  0.0 314.4 jit_solution(10559324621815543435)
XLA Ops:
  8.7 2.9 collective-permute-start.1
  11.6 2.4 collective-permute-done.1
  14.1 2.9 collective-permute-start.2
  20.3 44.0 %all-reduce.5.cloned.1.call-done = f32[128,128]{1,0:T(8,128)} async-done(((f32[128,128]{1,0:T(8,128)}), f32[128,128]{1,0:T(8,128)}) %all-reduce.5.cloned.1.call-update) | async-done | bytes 65552 | tf_op jit(solution)/shard_map/psum | solution.py:11
  68.0 3.8 %collective-permute-done.4 = f32[128,128]{1,0:T(8,128)S(1)} collective-permute-done((f32[128,128]{1,0:T(8,128)S(1)}, f32[128,128]{1,0:T(8,128)S(1)}, u32[]{:S(2)}, u32[]{:S(2)}) %collective-permute-start.4) | collective-permute-done | bytes 65568 | tf_op jit(solution)/shard_map/ppermute | solution.py:39
  71.9 1.4 collective-permute-start.5
  73.3 4.4 %collective-permute-done.5 = f32[128,128]{1,0:T(8,128)S(1)} collective-permute-done((f32[128,128]{1,0:T(8,128)S(1)}, f32[128,128]{1,0:T(8,128)S(1)}, u32[]{:S(2)}, u32[]{:S(2)}) %collective-permute-start.5) | collective-permute-done | bytes 65568 | tf_op jit(solution)/shard_map/ppermute | solution.py:39
  77.7 1.7 fusion.2
  79.5 41.0 %all-reduce.7.cloned.1.call-done = f32[128,128]{1,0:T(8,128)} async-done(((f32[128,128]{1,0:T(8,128)}), f32[128,128]{1,0:T(8,128)}) %all-reduce.7.cloned.1.call-update) | async-done | bytes 65552 | tf_op jit(solution)/shard_map/psum | solution.py:11
  122.6 2.7 collective-permute-start.7
  125.2 2.4 collective-permute-done.7
  127.7 1.7 collective-permute-start.8
  129.4 3.5 %collective-permute-done.8 = f32[128,128]{1,0:T(8,128)S(1)} collective-permute-done((f32[128,128]{1,0:T(8,128)S(1)}, f32[128,128]{1,0:T(8,128)S(1)}, u32[]{:S(2)}, u32[]{:S(2)}) %collective-permute-start.8) | collective-permute-done | bytes 65568 | tf_op jit(solution)/shard_map/ppermute | solution.py:39
  133.8 41.9 %all-reduce.9.cloned.1.call-done = f32[128,128]{1,0:T(8,128)} async-done(((f32[128,128]{1,0:T(8,128)}), f32[128,128]{1,0:T(8,128)}) %all-reduce.9.cloned.1.call-update) | async-done | bytes 65552 | tf_op jit(solution)/shard_map/psum | solution.py:11
  177.7 1.6 collective-permute-start.10
  179.3 2.8 collective-permute-done.10
  182.1 3.6 %collective-permute-start.11 = (f32[128,128]{1,0:T(8,128)S(1)}, f32[128,128]{1,0:T(8,128)S(1)}, u32[]{:S(2)}, u32[]{:S(2)}) collective-permute-start(f32[128,128]{1,0:T(8,128)S(1)} %add.83), channel_id=1, source_target_pairs={{0,4},{1,5},{2,6},{3,7},{4,0},{5,1},{6,2},{7,3},{8,12},{9,13},{10,... | collective-permute-start | bytes 196616 | tf_op jit(solution)/shard_map/ppermute | solution.py:39
  185.7 2.9 collective-permute-done.11
  189.5 40.8 %all-reduce.11.cloned.1.call-done = f32[128,128]{1,0:T(8,128)} async-done(((f32[128,128]{1,0:T(8,128)}), f32[128,128]{1,0:T(8,128)}) %all-reduce.11.cloned.1.call-update) | async-done | bytes 65552 | tf_op jit(solution)/shard_map/psum | solution.py:11
  231.2 1.8 convolution_bitcast_fusion
  233.0 36.1 %reduce-scatter.2.cloned.1.call-done = f32[1,512,128]{1,2,0:T(8,128)} async-done(((f32[8,512,128]{1,2,0:T(8,128)}), f32[1,512,128]{1,2,0:T(8,128)}) %reduce-scatter.2.cloned.1.call-update) | async-done | bytes 262160 | tf_op jit(solution)/shard_map/reduce_scatter | solution.py:66
  270.7 11.7 %custom-call.8 = f32[1,128,128]{2,1,0:T(8,128)S(1)} custom-call(f32[1,128,128]{2,1,0:T(8,128)S(1)} %fusion.10), custom_call_target="Cholesky" | custom-call | tf_op jit(solution)/shard_map/jit(cholesky)/cholesky | solution.py:19
  283.7 9.8 %custom-call.9 = f32[1,1,128,128]{2,3,1,0:T(8,128)S(1)} custom-call(f32[1,1,128,128]{3,2,1,0:T(8,128)S(1)} %fusion.9), custom_call_target="InvertDiagBlocksLowerTriangular" | custom-call | tf_op jit(solution)/shard_map/vmap(jit(_solve_triangular))/triangular_solve | solution.py:15
  295.0 12.1 %all_to_all.12 = f32[1,512,128]{2,0,1:T(1,128)S(1)} all-to-all(f32[1,512,128]{2,0,1:T(1,128)S(1)} %copy.53), channel_id=1, replica_groups=mesh['row'=4,'col'=8] {'col'}, dimensions={1} | all-to-all | bytes 524288 | tf_op jit(solution)/shard_map/all_to_all | solution.py:74
  (61 shorter events, 21.4 us)
Async XLA Ops:
  7.2 12.2 %copy-start = (f32[128,128]{1,0:T(8,128)S(1)}, f32[128,128]{1,0:T(8,128)}, u32[]{:S(2)}) copy-start(f32[128,128]{1,0:T(8,128)} %param.12) | copy-start | bytes 196612
  7.2 125.7 %copy-start.1 = (f32[128,128]{1,0:T(8,128)S(1)}, f32[128,128]{1,0:T(8,128)}, u32[]{:S(2)}) copy-start(f32[128,128]{1,0:T(8,128)} %param.10) | copy-start | bytes 196612
  7.2 57.1 %all-reduce.5.cloned.1.call-start = ((), (), s32[]{:S(2)}) async-start(), calls=%async_computation.2 | async-start | bytes 131072 | tf_op jit(solution)/shard_map/psum | solution.py:11
  7.3 223.9 %copy-start.2 = (bf16[64,4096]{1,0:T(8,128)(2,1)S(1)}, bf16[64,4096]{1,0:T(8,128)(2,1)}, u32[]{:S(2)}) copy-start(bf16[64,4096]{1,0:T(8,128)(2,1)} %param.13) | copy-start | bytes 1572868
  7.3 1.5 collective-permute-start
  8.7 5.3 %collective-permute-start.1 = (f32[128,128]{0,1:T(8,128)S(1)}, f32[128,128]{0,1:T(8,128)S(1)}, u32[]{:S(2)}, u32[]{:S(2)}) collective-permute-start(f32[128,128]{0,1:T(8,128)S(1)} %collective-permute-done), channel_id=1, source_target_pairs={{0,2},{1,3},{2,0},{3,1},{4,6},{5,7},{6,4},{7,5},{8,10},{9,11},{10,... | collective-permute-start | bytes 196616 | tf_op jit(solution)/shard_map/ppermute | solution.py:39
  14.1 5.3 %collective-permute-start.2 = (f32[128,128]{0,1:T(8,128)S(1)}, f32[128,128]{0,1:T(8,128)S(1)}, u32[]{:S(2)}, u32[]{:S(2)}) collective-permute-start(f32[128,128]{0,1:T(8,128)S(1)} %add.72), channel_id=1, source_target_pairs={{0,4},{1,5},{2,6},{3,7},{4,0},{5,1},{6,2},{7,3},{8,12},{9,13},{10,... | collective-permute-start | bytes 196616 | tf_op jit(solution)/shard_map/ppermute | solution.py:39
  20.2 100.2 %all-reduce.7.cloned.1.call-start = ((), (), s32[]{:S(2)}) async-start(), calls=%async_computation.3 | async-start | bytes 131072 | tf_op jit(solution)/shard_map/psum | solution.py:11
  64.3 166.0 %copy-start.4 = (f32[128,128]{1,0:T(8,128)S(1)}, f32[128,128]{1,0:T(8,128)}, u32[]{:S(2)}) copy-start(f32[128,128]{1,0:T(8,128)} %all-reduce.5.cloned.1.call-done) | copy-start | bytes 196612
  66.2 1.3 collective-permute-start.3
  67.5 4.3 %collective-permute-start.4 = (f32[128,128]{1,0:T(8,128)S(1)}, f32[128,128]{1,0:T(8,128)S(1)}, u32[]{:S(2)}, u32[]{:S(2)}) collective-permute-start(f32[128,128]{1,0:T(8,128)S(1)} %add.76), channel_id=1, source_target_pairs={{0,2},{1,3},{2,0},{3,1},{4,6},{5,7},{6,4},{7,5},{8,10},{9,11},{10,... | collective-permute-start | bytes 196616 | tf_op jit(solution)/shard_map/ppermute | solution.py:39
  71.9 5.8 %collective-permute-start.5 = (f32[128,128]{1,0:T(8,128)S(1)}, f32[128,128]{1,0:T(8,128)S(1)}, u32[]{:S(2)}, u32[]{:S(2)}) collective-permute-start(f32[128,128]{1,0:T(8,128)S(1)} %add.77), channel_id=1, source_target_pairs={{0,4},{1,5},{2,6},{3,7},{4,0},{5,1},{6,2},{7,3},{8,12},{9,13},{10,... | collective-permute-start | bytes 196616 | tf_op jit(solution)/shard_map/ppermute | solution.py:39
  79.4 96.3 %all-reduce.9.cloned.1.call-start = ((), (), s32[]{:S(2)}) async-start(), calls=%async_computation.4 | async-start | bytes 131072 | tf_op jit(solution)/shard_map/psum | solution.py:11
  120.5 109.9 %copy-start.5 = (f32[128,128]{1,0:T(8,128)S(1)}, f32[128,128]{1,0:T(8,128)}, u32[]{:S(2)}) copy-start(f32[128,128]{1,0:T(8,128)} %all-reduce.7.cloned.1.call-done) | copy-start | bytes 196612
  121.3 1.3 collective-permute-start.6
  122.6 5.1 %collective-permute-start.7 = (f32[128,128]{1,0:T(8,128)S(1)}, f32[128,128]{1,0:T(8,128)S(1)}, u32[]{:S(2)}, u32[]{:S(2)}) collective-permute-start(f32[128,128]{1,0:T(8,128)S(1)} %add.79), channel_id=1, source_target_pairs={{0,2},{1,3},{2,0},{3,1},{4,6},{5,7},{6,4},{7,5},{8,10},{9,11},{10,... | collective-permute-start | bytes 196616 | tf_op jit(solution)/shard_map/ppermute | solution.py:39
  127.7 5.3 %collective-permute-start.8 = (f32[128,128]{1,0:T(8,128)S(1)}, f32[128,128]{1,0:T(8,128)S(1)}, u32[]{:S(2)}, u32[]{:S(2)}) collective-permute-start(f32[128,128]{1,0:T(8,128)S(1)} %add.80), channel_id=1, source_target_pairs={{0,4},{1,5},{2,6},{3,7},{4,0},{5,1},{6,2},{7,3},{8,12},{9,13},{10,... | collective-permute-start | bytes 196616 | tf_op jit(solution)/shard_map/ppermute | solution.py:39
  133.8 96.5 %all-reduce.11.cloned.1.call-start = ((), (), s32[]{:S(2)}) async-start(), calls=%async_computation.5 | async-start | bytes 131072 | tf_op jit(solution)/shard_map/psum | solution.py:11
  176.5 1.3 collective-permute-start.9
  177.7 4.3 %collective-permute-start.10 = (f32[128,128]{1,0:T(8,128)S(1)}, f32[128,128]{1,0:T(8,128)S(1)}, u32[]{:S(2)}, u32[]{:S(2)}) collective-permute-start(f32[128,128]{1,0:T(8,128)S(1)} %add.82), channel_id=1, source_target_pairs={{0,2},{1,3},{2,0},{3,1},{4,6},{5,7},{6,4},{7,5},{8,10},{9,11},{10,... | collective-permute-start | bytes 196616 | tf_op jit(solution)/shard_map/ppermute | solution.py:39
  182.1 6.5 %collective-permute-start.11 = (f32[128,128]{1,0:T(8,128)S(1)}, f32[128,128]{1,0:T(8,128)S(1)}, u32[]{:S(2)}, u32[]{:S(2)}) collective-permute-start(f32[128,128]{1,0:T(8,128)S(1)} %add.83), channel_id=1, source_target_pairs={{0,4},{1,5},{2,6},{3,7},{4,0},{5,1},{6,2},{7,3},{8,12},{9,13},{10,... | collective-permute-start | bytes 196616 | tf_op jit(solution)/shard_map/ppermute | solution.py:39
  189.5 79.7 %reduce-scatter.2.cloned.1.call-start = ((), (), s32[]{:S(2)}) async-start(), calls=%async_computation.6 | async-start | bytes 2359296 | tf_op jit(solution)/shard_map/reduce_scatter | solution.py:66
  231.1 1.8 copy-start.3
Sparse Core Ops, SparseCore 0:
  20.4 43.8 all-reduce.4
  79.5 40.8 all-reduce.6
  133.9 41.7 all-reduce.8
  189.6 40.6 all-reduce.10
  233.1 35.9 reduce-scatter.1
